TPU v7x, 32 devices: a whole 2x2x4 slice. The times are simulated.
32 devices in a mesh: row: 4 (over z), col: 8 (over y, x, core).
Axes of the slice: x: 2, y: 2, z: 4, core: 2. Of those that a mesh axis runs over, the one named last changes fastest.
Arguments:
- trailing: float32 [16384, 3072], P('row', 'col'), may hold values from -6 to 6
- leaf_vectors: float32 [16384, 256], P(('row', 'col')), may hold values from -1 to 1, as said below
- leaf_factor: float32 [1024, 256], P(('row', 'col')), may hold values from -1 to 2, as said below
- tree_vectors: float32 [1024, 256], P(('row', 'col')), may hold values from -1 to 1, as said below
- tree_factor: float32 [1024, 256], P(('row', 'col')), may hold values from -1 to 2, as said below
Outputs:
- updated: float32 [16384, 3072], P('row', 'col')
Inputs may be any that keep to these rules, and one draw needn't show every extreme that they name: `leaf_vectors`: in each row block of 4096 rows, row r < 256 of the block holds 1 in column r and 0 in every column after r. `leaf_factor`: each 256 x 256 block is upper triangular with its diagonal between 1 and 2. `tree_vectors`: each 256 x 256 block is upper triangular. `tree_factor`: each 256 x 256 block is upper triangular with its diagonal between 1 and 2.
All inputs are finite; a program needn't handle non-finite values.
Results may differ from a plain program's by a relative error of at most 0.0002.
Values sent between devices are 32-bit elements; how exact they have to be, the bound alone decides.
No kernel may reach another device: no remote copies, remote signals or barrier semaphores. Data moves between devices by JAX's collectives and lax.ppermute only.
A program may use at most 128 MiB of HBM per device.

v0:
```python
import jax
import jax.numpy as jnp
from jax import lax
from jax.sharding import PartitionSpec as P

highest = lax.Precision.HIGHEST
contract_rows = (((0,), (0,)), ((), ()))


def swapped(array, axis, apart):
    return lax.ppermute(array, axis, [(i, i ^ 1 << apart) for i in range(lax.axis_size(axis))])


def left_product(first, second):
    return lax.dot_general(
        first, second, contract_rows, precision=highest, preferred_element_type=jnp.float32
    )


def plain_product(first, second):
    return jnp.dot(first, second, precision=highest, preferred_element_type=jnp.float32)


def shards(trailing, leaf_vectors, leaf_factor, tree_vectors, tree_factor):
    panel_width = leaf_factor.shape[1]
    panel, block_factor, own_vectors, own_factor = (
        lax.all_gather(leaf_vectors, "col", axis=0, tiled=True),
        lax.all_gather(leaf_factor, "col", axis=0, tiled=True),
        lax.all_gather(tree_vectors, "col", axis=0, tiled=True),
        lax.all_gather(tree_factor, "col", axis=0, tiled=True),
    )
    weights = left_product(block_factor, left_product(panel, trailing))
    updated = trailing - plain_product(panel, weights)
    upper_rows = updated[:panel_width]
    lower_rows = updated[panel_width:]
    sections = lax.axis_size("row").bit_length() - 1
    position = lax.axis_index("row")
    pair_vectors, pair_factor = (
        lax.all_gather(own_vectors, "row", axis=0, tiled=True),
        lax.all_gather(own_factor, "row", axis=0, tiled=True),
    )
    current = upper_rows
    final_top = upper_rows
    for level_bit in range(sections):
        stride = 1 << level_bit
        partner_top = swapped(current, "row", level_bit)
        on_upper = position // stride % 2 == 1
        lower_group = jnp.where(on_upper, partner_top, current)
        upper_group = jnp.where(on_upper, current, partner_top)
        chosen = position // (2 * stride) * (2 * stride) + stride
        vectors = lax.dynamic_slice_in_dim(pair_vectors, chosen * panel_width, panel_width, 0)
        factor = lax.dynamic_slice_in_dim(pair_factor, chosen * panel_width, panel_width, 0)
        tree_weights = left_product(factor, lower_group + left_product(vectors, upper_group))
        final_top = jnp.where(
            position % (2 * stride) == stride,
            upper_group - plain_product(vectors, tree_weights),
            final_top,
        )
        current = lower_group - tree_weights
    final_top = jnp.where(position == 0, current, final_top)
    return jnp.concatenate([final_top, lower_rows], 0)


def solution(mesh):
    placed = (
        P("row", "col"),
        P(("row", "col"), None),
        P(("row", "col"), None),
        P(("row", "col"), None),
        P(("row", "col"), None),
    )
    return jax.shard_map(
        shards, mesh=mesh, in_specs=placed, out_specs=P("row", "col"), check_vma=False
    )
```

profile of v0, /device:TPU:0, one launch (start us, length us, event | category | flops | bytes accessed | tf_op | source)
XLA Modules:
  0.0 161.5 jit_solution(10669404419144354708)
XLA Ops:
  6.5 0.0 all-gather.4.cloned.1.call-start
  6.5 0.7 all-gather.4.cloned.1.call-update
  7.3 0.0 all-gather.8.cloned.1.call-start
  7.3 12.6 %all_gather.22 = f32[256,256]{1,0:T(8,128)} all-gather(f32[32,256]{1,0:T(8,128)} %param.8), channel_id=1, replica_groups=mesh['row'=4,'col'=8] {'col'}, dimensions={0}, use_global_device_ids=true | all-gather | bytes 294912 | tf_op jit(solution)/shard_map/all_gather | solution.py:29
  19.9 0.0 all-gather.8.cloned.1.call-update
  19.9 0.0 all-gather.6.cloned.1.call-start
  20.0 10.6 %all_gather.20 = f32[256,256]{1,0:T(8,128)} all-gather(f32[32,256]{1,0:T(8,128)} %param.9), channel_id=1, replica_groups=mesh['row'=4,'col'=8] {'col'}, dimensions={0}, use_global_device_ids=true | all-gather | bytes 294912 | tf_op jit(solution)/shard_map/all_gather | solution.py:30
  30.6 0.0 all-gather.6.cloned.1.call-update
  30.6 9.8 %all_gather.19 = f32[256,256]{1,0:T(8,128)S(1)} all-gather(f32[32,256]{1,0:T(8,128)} %param.7), channel_id=1, replica_groups=mesh['row'=4,'col'=8] {'col'}, dimensions={0}, use_global_device_ids=true | all-gather | bytes 294912 | tf_op jit(solution)/shard_map/all_gather | solution.py:28
  40.4 6.6 %copy.6 = f32[4096,384]{0,1:T(8,128)} copy(f32[4096,384]{1,0:T(8,128)} %param.5) | data formatting | bytes 12582912 | tf_op args[0]
  47.0 3.2 %all-gather.4.cloned.1.call-done = f32[4096,256]{1,0:T(8,128)} async-done(((f32[512,256]{1,0:T(8,128)}), f32[4096,256]{1,0:T(8,128)}) %all-gather.4.cloned.1.call-update) | async-done | bytes 4194320 | tf_op jit(solution)/shard_map/all_gather | solution.py:27
  50.2 0.0 copy-start.1
  50.2 0.0 copy-start.2
  50.2 9.9 %fusion.20 = f32[256,384]{1,0:T(8,128)S(1)} fusion(f32[4096,256]{1,0:T(8,128)} %all-gather.4.cloned.1.call-done, f32[4096,384]{1,0:T(8,128)} %param.5), kind=kOutput, calls=%fused_computation.29 | convolution fusion | flops 4831838208 | bytes 10878976 | tf_op jit(solution)/shard_map/dot_general | solution.py:15
  60.2 0.8 fusion.21
  61.0 0.0 copy-done.1
  61.0 0.0 copy-done.2
  61.0 6.0 %bitcast_subtract_fusion = f32[4096,384]{0,1:T(8,128)S(1)} fusion(f32[4096,384]{0,1:T(8,128)S(1)} %copy-done.1, f32[384,256]{1,0:T(8,128)S(1)} %fusion.21, f32[4096,256]{1,0:T(8,128)S(1)} %copy-done.2), kind=kOutput, calls=%fused_computation.1 | convolution fusion | flops 4833411072 | bytes 17170432 | tf_op jit(solution)/shard_map/dot_general | solution.py:21
  67.0 0.0 copy-start
  67.0 2.7 %copy-done = f32[4096,384]{0,1:T(8,128)} copy-done((f32[4096,384]{0,1:T(8,128)}, f32[4096,384]{0,1:T(8,128)S(1)}, u32[]{:S(2)}) %copy-start) | copy-done | bytes 6291480
  69.8 1.5 collective-permute-start
  71.3 10.8 %all-gather.8.cloned.1.call-done = f32[1024,256]{1,0:T(8,128)} async-done(((f32[256,256]{1,0:T(8,128)}), f32[1024,256]{1,0:T(8,128)}) %all-gather.8.cloned.1.call-update) | async-done | bytes 1048592 | tf_op jit(solution)/shard_map/all_gather | solution.py:39
  82.1 5.2 %collective-permute-done = f32[256,384]{0,1:T(8,128)S(1)} collective-permute-done((f32[256,384]{0,1:T(8,128)S(1)}, f32[256,384]{0,1:T(8,128)S(1)}, u32[]{:S(2)}, u32[]{:S(2)}) %collective-permute-start) | collective-permute-done | bytes 393248 | tf_op jit(solution)/shard_map/ppermute | solution.py:11
  87.3 1.7 %convolution_add_fusion.1 = f32[256,384]{0,1:T(8,128)S(1)} fusion(f32[1024,256]{1,0:T(8,128)} %all-gather.8.cloned.1.call-done, s32[]{:T(128)S(6)} %select_n.79, f32[256,384]{0,1:T(8,128)S(1)} %collective-permute-done, pred[]{:T(512)S(6)} %eq.20, f32[4096,384]{0,1:T(8,128)} %copy-done), kind=kOutput, calls=%fused_computation.7 | convolution fusion | flops 302284800 | bytes 2229760 | tf_op jit(solution)/shard_map/dot_general | solution.py:15
  89.0 26.9 %all-gather.6.cloned.1.call-done = f32[1024,256]{1,0:T(8,128)} async-done(((f32[256,256]{1,0:T(8,128)}), f32[1024,256]{1,0:T(8,128)}) %all-gather.6.cloned.1.call-update) | async-done | bytes 1048592 | tf_op jit(solution)/shard_map/all_gather | solution.py:40
  115.9 2.0 %fusion.4 = f32[256,384]{1,0:T(8,128)S(1)} fusion(f32[256,384]{0,1:T(8,128)S(1)} %convolution_add_fusion.1, f32[1024,256]{1,0:T(8,128)} %all-gather.6.cloned.1.call-done, s32[]{:T(128)S(6)} %select_n.79), kind=kOutput, calls=%fused_computation.11 | convolution fusion | flops 301989888 | bytes 1048580 | tf_op jit(solution)/shard_map/dot_general | solution.py:15
  117.9 0.2 copy.7
  118.0 1.1 fusion.12
  119.1 0.0 copy-start.3
  119.1 1.9 %collective-permute-start.1 = (f32[256,384]{0,1:T(8,128)S(1)}, f32[256,384]{0,1:T(8,128)S(1)}, u32[]{:S(2)}, u32[]{:S(2)}) collective-permute-start(f32[256,384]{0,1:T(8,128)S(1)} %fusion.12), channel_id=1, source_target_pairs={{0,16},{8,24},{16,0},{24,8},{1,17},{9,25},{17,1},{25,9},{2,18},{10... | collective-permute-start | bytes 1179656 | tf_op jit(solution)/shard_map/ppermute | solution.py:11
  121.0 5.6 %slice.9 = f32[3840,384]{0,1:T(8,128)} slice(f32[4096,384]{0,1:T(8,128)} %copy-done), slice={[256:4096], [0:384]} | slice | bytes 11796480 | tf_op jit(solution)/shard_map/slice | solution.py:35
  126.6 0.0 copy-done.3
  126.6 1.8 %fusion = f32[256,384]{0,1:T(8,128)S(1)} fusion(f32[256,384]{1,0:T(8,128)S(1)} %fusion.4, f32[1024,256]{1,0:T(8,128)S(1)} %copy-done.3, s32[]{:T(128)S(6)} %select_n.79, pred[]{:T(512)S(6)} %eq.20, f32[256,384]{0,1:T(8,128)S(1)} %collective-permute-done, f32[4096,384]{0,1:T(8,128)} %copy-done), kind=kOutput, calls=%fused_computation.3 | convolution fusion | flops 302284800 | bytes 1835013 | tf_op jit(solution)/shard_map/dot_general | solution.py:21
  128.4 10.5 %collective-permute-done.1 = f32[256,384]{0,1:T(8,128)S(1)} collective-permute-done((f32[256,384]{0,1:T(8,128)S(1)}, f32[256,384]{0,1:T(8,128)S(1)}, u32[]{:S(2)}, u32[]{:S(2)}) %collective-permute-start.1) | collective-permute-done | bytes 393248 | tf_op jit(solution)/shard_map/ppermute | solution.py:11
  138.9 0.5 convolution_add_fusion
  139.4 2.0 %fusion.2 = f32[256,384]{1,0:T(8,128)S(1)} fusion(f32[256,384]{0,1:T(8,128)S(1)} %convolution_add_fusion, f32[1024,256]{1,0:T(8,128)} %all-gather.6.cloned.1.call-done, s32[]{:T(128)S(6)} %select_n.83), kind=kOutput, calls=%fused_computation.9 | convolution fusion | flops 301989888 | bytes 1048580 | tf_op jit(solution)/shard_map/dot_general | solution.py:15
  141.4 0.2 copy.8
  141.6 0.8 subtract_select_fusion
  142.4 6.0 %pad_maximum_fusion = f32[4096,384]{0,1:T(8,128)} fusion(f32[3840,384]{0,1:T(8,128)} %slice.9, f32[256,384]{0,1:T(8,128)S(1)} %subtract_select_fusion), kind=kLoop, calls=%fused_computation | loop fusion | flops 1572864 | bytes 12582912 | tf_op jit(solution)/shard_map/concatenate | solution.py:61
  148.5 6.6 %copy.11 = f32[4096,384]{1,0:T(8,128)} copy(f32[4096,384]{0,1:T(8,128)} %pad_maximum_fusion) | data formatting | bytes 12582912 | tf_op jit(solution)/shard_map/concatenate | solution.py:61
  (1 shorter events, 0.0 us)
Async XLA Ops:
  6.5 43.7 %all-gather.4.cloned.1.call-start = ((), (), s32[]{:S(2)}) async-start(), calls=%async_computation | async-start | bytes 4718592 | tf_op jit(solution)/shard_map/all_gather | solution.py:27
  7.3 74.9 %all-gather.8.cloned.1.call-start = ((), (), s32[]{:S(2)}) async-start(), calls=%async_computation.2 | async-start | bytes 1310720 | tf_op jit(solution)/shard_map/all_gather | solution.py:39
  19.9 96.0 %all-gather.6.cloned.1.call-start = ((), (), s32[]{:S(2)}) async-start(), calls=%async_computation.1 | async-start | bytes 1310720 | tf_op jit(solution)/shard_map/all_gather | solution.py:40
  50.2 10.7 %copy-start.1 = (f32[4096,384]{0,1:T(8,128)S(1)}, f32[4096,384]{0,1:T(8,128)}, u32[]{:S(2)}) copy-start(f32[4096,384]{0,1:T(8,128)} %copy.6) | copy-start | bytes 18874372
  50.2 10.7 %copy-start.2 = (f32[4096,256]{1,0:T(8,128)S(1)}, f32[4096,256]{1,0:T(8,128)}, u32[]{:S(2)}) copy-start(f32[4096,256]{1,0:T(8,128)} %all-gather.4.cloned.1.call-done) | copy-start | bytes 12582916
  67.0 2.7 %copy-start = (f32[4096,384]{0,1:T(8,128)}, f32[4096,384]{0,1:T(8,128)S(1)}, u32[]{:S(2)}) copy-start(f32[4096,384]{0,1:T(8,128)S(1)} %bitcast_subtract_fusion) | copy-start | bytes 18874372
  69.8 17.5 %collective-permute-start = (f32[256,384]{0,1:T(8,128)S(1)}, f32[256,384]{0,1:T(8,128)S(1)}, u32[]{:S(2)}, u32[]{:S(2)}) collective-permute-start(f32[256,384]{0,1:T(8,128)S(1)} %slice.8), channel_id=1, source_target_pairs={{0,8},{8,0},{16,24},{24,16},{1,9},{9,1},{17,25},{25,17},{2,10},{10... | collective-permute-start | bytes 1179656 | tf_op jit(solution)/shard_map/ppermute | solution.py:11
  119.1 7.4 %copy-start.3 = (f32[1024,256]{1,0:T(8,128)S(1)}, f32[1024,256]{1,0:T(8,128)}, u32[]{:S(2)}) copy-start(f32[1024,256]{1,0:T(8,128)} %all-gather.8.cloned.1.call-done) | copy-start | bytes 3145732
  119.1 19.8 %collective-permute-start.1 = (f32[256,384]{0,1:T(8,128)S(1)}, f32[256,384]{0,1:T(8,128)S(1)}, u32[]{:S(2)}, u32[]{:S(2)}) collective-permute-start(f32[256,384]{0,1:T(8,128)S(1)} %fusion.12), channel_id=1, source_target_pairs={{0,16},{8,24},{16,0},{24,8},{1,17},{9,25},{17,1},{25,9},{2,18},{10... | collective-permute-start | bytes 1179656 | tf_op jit(solution)/shard_map/ppermute | solution.py:11
Sparse Core Ops, SparseCore 0:
  9.2 40.9 all-gather.3
  51.8 30.2 all-gather.7
  83.7 32.1 all-gather.5
where the time goes:
time: 162 us
  waiting for transfers between devices  57.4 us (35%)
  blocking collectives  33 us (20%)
  matrix products  25.5 us (16%)
  local copies, waits for them, and re-layouts  21.8 us (13%)
  between operations  13.2 us (8%)
  other arithmetic  7.11 us (4%)
  starting transfers between devices  3.49 us (2%)
    all_gather x1, waiting for transfers between devices, shards(): lax.all_gather(own_factor, 'row', axis=0, tiled=True)  26.9 us
    dot_general x6, matrix products, left_product(): lax.dot_general(first, second, contract_rows, precision=highest, preferre...  16.9 us
    ppermute x2, waiting for transfers between devices, swapped(): lax.ppermute(array, axis, [(i, i ^ 1 << apart) for i in range(lax.axis_si...  15.7 us
    all_gather x1, blocking collectives, shards(): lax.all_gather(tree_vectors, 'col', axis=0, tiled=True)  12.6 us
    all_gather x1, waiting for transfers between devices, shards(): lax.all_gather(own_vectors, 'row', axis=0, tiled=True)  10.8 us
    all_gather x1, blocking collectives, shards(): lax.all_gather(tree_factor, 'col', axis=0, tiled=True)  10.6 us
    all_gather x1, blocking collectives, shards(): lax.all_gather(leaf_factor, 'col', axis=0, tiled=True)  9.82 us
    unnamed x9, local copies, waits for them, and re-layouts  9.34 us
  transfers between devices with their start and end apart: 5, of which 5 were waited for; matrix products, arithmetic and copies ran while one was open for 20% of the time, Pallas kernels for 0%

commit v1 on v0

--- a/solution.py
+++ b/solution.py
@@ -5,6 +5,28 @@
 
 highest = lax.Precision.HIGHEST
 contract_rows = (((0,), (0,)), ((), ()))
+
+
+def in_order(blocks, dim):
+    blocks = jnp.moveaxis(blocks, 0, dim)
+    shape = blocks.shape
+    return blocks.reshape(*shape[:dim], shape[dim] * shape[dim + 1], *shape[dim + 2 :])
+
+
+def grow_blocks(value, axis):
+    size = lax.axis_size(axis)
+    blocks = value[None]
+    for level in range(size.bit_length() - 1):
+        bit = 1 << level
+        other = lax.ppermute(blocks, axis, [(i, i ^ bit) for i in range(size)])
+        both = jnp.stack([blocks, other])
+        upper = lax.axis_index(axis) >> level & 1
+        blocks = jnp.where(upper == 0, both, both[::-1]).reshape(-1, *value.shape)
+    return blocks
+
+
+def collect(shard, axis, dim):
+    return in_order(grow_blocks(shard, axis), dim)
 
 
 def swapped(array, axis, apart):
@@ -37,7 +59,7 @@
     position = lax.axis_index("row")
     pair_vectors, pair_factor = (
         lax.all_gather(own_vectors, "row", axis=0, tiled=True),
-        lax.all_gather(own_factor, "row", axis=0, tiled=True),
+        collect(own_factor, "row", 0),
     )
     current = upper_rows
     final_top = upper_rows

time: 162 us -> 146 us (0.901)
  waiting for transfers between devices: 57.4 us -> 38.1 us
  starting transfers between devices: 3.49 us -> 6.16 us
    all_gather x1 -> x0, waiting for transfers between devices: 26.9 us -> none  [shards(): lax.all_gather(own_factor, 'row', axis=0, tiled=True)]
    ppermute x0 -> x2, waiting for transfers between devices: none -> 17.4 us  [grow_blocks(): other = lax.ppermute(blocks, axis, [(i, i ^ bit) for i in range(size)])]
    all_gather x1, waiting for transfers between devices: 10.8 us -> 2.01 us  [shards(): lax.all_gather(own_vectors, 'row', axis=0, tiled=True)]
    ppermute x0 -> x2, starting transfers between devices: none -> 4.06 us  [grow_blocks(): other = lax.ppermute(blocks, axis, [(i, i ^ bit) for i in range(size)])]
    dot_general x3, matrix products: 8.63 us -> 11.7 us  [plain_product(): jnp.dot(first, second, precision=highest, preferred_element_type=jnp.floa...]
    all_gather x1, waiting for transfers between devices: 3.21 us -> 0.35 us  [shards(): lax.all_gather(leaf_vectors, 'col', axis=0, tiled=True)]
    all_gather x1, blocking collectives: 12.6 us -> 10.5 us  [shards(): lax.all_gather(tree_vectors, 'col', axis=0, tiled=True)]
    dot_general x6, matrix products: 16.9 us -> 14.8 us  [left_product(): lax.dot_general(first, second, contract_rows, precision=highest, preferre...]
  transfers between devices with their start and end apart: 5 -> 6, of which waited for: 5 -> 5; matrix products, arithmetic and copies ran while one was open for 20% -> 23% of each run, Pallas kernels for 0% -> 0%
where the time goes in v1:
time: 146 us
  waiting for transfers between devices  38.1 us (26%)
  blocking collectives  31.7 us (22%)
  matrix products  26.5 us (18%)
  local copies, waits for them, and re-layouts  22.3 us (15%)
  between operations  13.6 us (9%)
  other arithmetic  7.4 us (5%)
  starting transfers between devices  6.16 us (4%)
    ppermute x2, waiting for transfers between devices, swapped(): lax.ppermute(array, axis, [(i, i ^ 1 << apart) for i in range(lax.axis_si...  17.6 us
    ppermute x2, waiting for transfers between devices, grow_blocks(): other = lax.ppermute(blocks, axis, [(i, i ^ bit) for i in range(size)])  17.4 us
    dot_general x6, matrix products, left_product(): lax.dot_general(first, second, contract_rows, precision=highest, preferre...  14.8 us
    dot_general x3, matrix products, plain_product(): jnp.dot(first, second, precision=highest, preferred_element_type=jnp.floa...  11.7 us
    all_gather x1, blocking collectives, shards(): lax.all_gather(tree_factor, 'col', axis=0, tiled=True)  11 us
    all_gather x1, blocking collectives, shards(): lax.all_gather(tree_vectors, 'col', axis=0, tiled=True)  10.5 us
    all_gather x1, blocking collectives, shards(): lax.all_gather(leaf_factor, 'col', axis=0, tiled=True)  10.2 us
    unnamed x9, local copies, waits for them, and re-layouts  9.72 us
  transfers between devices with their start and end apart: 6, of which 5 were waited for; matrix products, arithmetic and copies ran while one was open for 23% of the time, Pallas kernels for 0%

profile of v1, /device:TPU:0, one launch (start us, length us, event | category | flops | bytes accessed | tf_op | source)
XLA Modules:
  0.0 145.8 jit_solution(5518111521581944324)
XLA Ops:
  6.5 0.0 all-gather.3.cloned.1.call-start
  6.5 0.7 all-gather.3.cloned.1.call-update
  7.3 0.0 all-gather.5.cloned.1.call-start
  7.3 11.0 %all_gather.17 = f32[256,256]{1,0:T(8,128)S(1)} all-gather(f32[32,256]{1,0:T(8,128)} %param.9), channel_id=1, replica_groups=mesh['row'=4,'col'=8] {'col'}, dimensions={0}, use_global_device_ids=true | all-gather | bytes 294912 | tf_op jit(solution)/shard_map/all_gather | solution.py:52
  18.3 1.6 %collective-permute-start.1 = (f32[1,256,256]{2,1,0:T(8,128)S(1)}, f32[1,256,256]{2,1,0:T(8,128)S(1)}, u32[]{:S(2)}, u32[]{:S(2)}) collective-permute-start(f32[1,256,256]{2,1,0:T(8,128)S(1)} %bitcast.23), channel_id=1, source_target_pairs={{0,8},{8,0},{16,24},{24,16},{1,9},{9,1},{17,25},{25,17},{2,10},{10... | collective-permute-start | bytes 786440 | tf_op jit(solution)/shard_map/ppermute | solution.py:21
  19.9 10.5 %all_gather.18 = f32[256,256]{1,0:T(8,128)} all-gather(f32[32,256]{1,0:T(8,128)} %param.8), channel_id=1, replica_groups=mesh['row'=4,'col'=8] {'col'}, dimensions={0}, use_global_device_ids=true | all-gather | bytes 294912 | tf_op jit(solution)/shard_map/all_gather | solution.py:51
  30.4 0.0 all-gather.5.cloned.1.call-update
  30.4 0.0 copy-start.3
  30.5 7.0 %copy.6 = f32[4096,384]{0,1:T(8,128)} copy(f32[4096,384]{1,0:T(8,128)} %param.5) | data formatting | bytes 12582912 | tf_op args[0]
  37.5 0.0 copy-done.3
  37.5 10.2 %all_gather.16 = f32[256,256]{1,0:T(8,128)S(1)} all-gather(f32[32,256]{1,0:T(8,128)S(1)} %copy-done.3), channel_id=1, replica_groups=mesh['row'=4,'col'=8] {'col'}, dimensions={0}, use_global_device_ids=true | all-gather | bytes 294912 | tf_op jit(solution)/shard_map/all_gather | solution.py:50
  47.7 0.0 collective-permute-done.1
  47.7 0.1 fusion.3
  47.8 2.5 %collective-permute-start.2 = (f32[2,256,256]{2,1,0:T(8,128)S(1)}, f32[2,256,256]{2,1,0:T(8,128)S(1)}, u32[]{:S(2)}, u32[]{:S(2)}) collective-permute-start(f32[2,256,256]{2,1,0:T(8,128)S(1)} %get-tuple-element.6), channel_id=1, source_target_pairs={{0,16},{8,24},{16,0},{24,8},{1,17},{9,25},{17,1},{25,9},{2,18},{10... | collective-permute-start | bytes 1572872 | tf_op jit(solution)/shard_map/ppermute | solution.py:21
  50.3 0.4 all-gather.3.cloned.1.call-done
  50.7 0.0 copy-start.1
  50.7 9.7 %fusion.22 = f32[256,384]{1,0:T(8,128)S(1)} fusion(f32[4096,256]{1,0:T(8,128)} %all-gather.3.cloned.1.call-done, f32[4096,384]{1,0:T(8,128)} %param.5), kind=kOutput, calls=%fused_computation.35 | convolution fusion | flops 4831838208 | bytes 10878976 | tf_op jit(solution)/shard_map/dot_general | solution.py:37
  60.4 0.8 fusion.23
  61.2 0.0 copy-done.1
  61.2 8.1 %bitcast_subtract_fusion = f32[4096,384]{0,1:T(8,128)S(1)} fusion(f32[4096,384]{0,1:T(8,128)} %copy.6, f32[384,256]{1,0:T(8,128)S(1)} %fusion.23, f32[4096,256]{1,0:T(8,128)S(1)} %copy-done.1), kind=kOutput, calls=%fused_computation.1 | convolution fusion | flops 4833411072 | bytes 17170432 | tf_op jit(solution)/shard_map/dot_general | solution.py:43
  69.3 0.0 copy-start
  69.3 2.7 %copy-done = f32[4096,384]{0,1:T(8,128)} copy-done((f32[4096,384]{0,1:T(8,128)}, f32[4096,384]{0,1:T(8,128)S(1)}, u32[]{:S(2)}) %copy-start) | copy-done | bytes 6291480
  72.1 1.6 %collective-permute-start = (f32[256,384]{0,1:T(8,128)S(1)}, f32[256,384]{0,1:T(8,128)S(1)}, u32[]{:S(2)}, u32[]{:S(2)}) collective-permute-start(f32[256,384]{0,1:T(8,128)S(1)} %slice.8), channel_id=1, source_target_pairs={{0,8},{8,0},{16,24},{24,16},{1,9},{9,1},{17,25},{25,17},{2,10},{10... | collective-permute-start | bytes 1179656 | tf_op jit(solution)/shard_map/ppermute | solution.py:33
  73.6 17.4 %collective-permute-done.2 = f32[2,256,256]{2,1,0:T(8,128)S(1)} collective-permute-done((f32[2,256,256]{2,1,0:T(8,128)S(1)}, f32[2,256,256]{2,1,0:T(8,128)S(1)}, u32[]{:S(2)}, u32[]{:S(2)}) %collective-permute-start.2) | collective-permute-done | bytes 524320 | tf_op jit(solution)/shard_map/ppermute | solution.py:21
  91.0 0.1 pad_maximum_fusion.1
  91.1 0.1 reverse_select_fusion
  91.2 2.0 %all-gather.5.cloned.1.call-done = f32[1024,256]{1,0:T(8,128)} async-done(((f32[256,256]{1,0:T(8,128)}), f32[1024,256]{1,0:T(8,128)}) %all-gather.5.cloned.1.call-update) | async-done | bytes 1048592 | tf_op jit(solution)/shard_map/all_gather | solution.py:61
  93.2 5.3 %collective-permute-done = f32[256,384]{0,1:T(8,128)S(1)} collective-permute-done((f32[256,384]{0,1:T(8,128)S(1)}, f32[256,384]{0,1:T(8,128)S(1)}, u32[]{:S(2)}, u32[]{:S(2)}) %collective-permute-start) | collective-permute-done | bytes 393248 | tf_op jit(solution)/shard_map/ppermute | solution.py:33
  98.5 1.7 %convolution_add_fusion.1 = f32[256,384]{0,1:T(8,128)S(1)} fusion(f32[1024,256]{1,0:T(8,128)} %all-gather.5.cloned.1.call-done, s32[]{:T(128)S(6)} %select_n.99, f32[256,384]{0,1:T(8,128)S(1)} %collective-permute-done, pred[]{:T(512)S(6)} %eq.26, f32[4096,384]{0,1:T(8,128)} %copy-done), kind=kOutput, calls=%fused_computation.8 | convolution fusion | flops 302284800 | bytes 2229760 | tf_op jit(solution)/shard_map/dot_general | solution.py:37
  100.2 1.1 fusion.6
  101.3 0.2 copy.7
  101.5 1.1 fusion.14
  102.6 0.5 collective-permute-start.3
  103.1 0.0 copy-start.2
  103.1 5.7 %slice.9 = f32[3840,384]{0,1:T(8,128)} slice(f32[4096,384]{0,1:T(8,128)} %copy-done), slice={[256:4096], [0:384]} | slice | bytes 11796480 | tf_op jit(solution)/shard_map/slice | solution.py:57
  108.7 0.0 copy-done.2
  108.7 1.8 %fusion = f32[256,384]{0,1:T(8,128)S(1)} fusion(f32[256,384]{1,0:T(8,128)S(1)} %fusion.6, f32[1024,256]{1,0:T(8,128)S(1)} %copy-done.2, s32[]{:T(128)S(6)} %select_n.99, pred[]{:T(512)S(6)} %eq.26, f32[256,384]{0,1:T(8,128)S(1)} %collective-permute-done, f32[4096,384]{0,1:T(8,128)} %copy-done), kind=kOutput, calls=%fused_computation.4 | convolution fusion | flops 302284800 | bytes 1835013 | tf_op jit(solution)/shard_map/dot_general | solution.py:43
  110.5 12.3 %collective-permute-done.3 = f32[256,384]{0,1:T(8,128)S(1)} collective-permute-done((f32[256,384]{0,1:T(8,128)S(1)}, f32[256,384]{0,1:T(8,128)S(1)}, u32[]{:S(2)}, u32[]{:S(2)}) %collective-permute-start.3) | collective-permute-done | bytes 393248 | tf_op jit(solution)/shard_map/ppermute | solution.py:33
  122.8 0.5 convolution_add_fusion
  123.3 1.1 fusion.4
  124.4 0.2 copy.8
  124.6 1.8 %subtract_select_fusion = f32[256,384]{0,1:T(8,128)S(1)} fusion(f32[256,384]{0,1:T(8,128)S(1)} %copy.8, f32[256,384]{0,1:T(8,128)S(1)} %fusion, f32[256,384]{1,0:T(8,128)S(1)} %fusion.4, f32[1024,256]{1,0:T(8,128)} %all-gather.5.cloned.1.call-done, s32[]{:T(128)S(6)} %select_n.103, pred[]{:T(512)S(6)} %eq.29, pred[]{:T(512)S(6)} %eq.24, ...), kind=kOutput, calls=%fused_computation.14 | convolution fusion | flops 302579712 | bytes 2621447 | tf_op jit(solution)/shard_map/dot_general | solution.py:43
  126.3 6.0 %pad_maximum_fusion = f32[4096,384]{0,1:T(8,128)} fusion(f32[3840,384]{0,1:T(8,128)} %slice.9, f32[256,384]{0,1:T(8,128)S(1)} %subtract_select_fusion), kind=kLoop, calls=%fused_computation | loop fusion | flops 1572864 | bytes 12582912 | tf_op jit(solution)/shard_map/concatenate | solution.py:83
  132.4 6.6 %copy.11 = f32[4096,384]{1,0:T(8,128)} copy(f32[4096,384]{0,1:T(8,128)} %pad_maximum_fusion) | data formatting | bytes 12582912 | tf_op jit(solution)/shard_map/concatenate | solution.py:83
  (2 shorter events, 0.1 us)
Async XLA Ops:
  6.5 44.1 %all-gather.3.cloned.1.call-start = ((), (), s32[]{:S(2)}) async-start(), calls=%async_computation | async-start | bytes 4718592 | tf_op jit(solution)/shard_map/all_gather | solution.py:49
  7.3 86.0 %all-gather.5.cloned.1.call-start = ((), (), s32[]{:S(2)}) async-start(), calls=%async_computation.1 | async-start | bytes 1310720 | tf_op jit(solution)/shard_map/all_gather | solution.py:61
  18.3 29.4 %collective-permute-start.1 = (f32[1,256,256]{2,1,0:T(8,128)S(1)}, f32[1,256,256]{2,1,0:T(8,128)S(1)}, u32[]{:S(2)}, u32[]{:S(2)}) collective-permute-start(f32[1,256,256]{2,1,0:T(8,128)S(1)} %bitcast.23), channel_id=1, source_target_pairs={{0,8},{8,0},{16,24},{24,16},{1,9},{9,1},{17,25},{25,17},{2,10},{10... | collective-permute-start | bytes 786440 | tf_op jit(solution)/shard_map/ppermute | solution.py:21
  30.4 7.0 %copy-start.3 = (f32[32,256]{1,0:T(8,128)S(1)}, f32[32,256]{1,0:T(8,128)}, u32[]{:S(2)}) copy-start(f32[32,256]{1,0:T(8,128)} %param.7) | copy-start | bytes 98308
  47.8 43.2 %collective-permute-start.2 = (f32[2,256,256]{2,1,0:T(8,128)S(1)}, f32[2,256,256]{2,1,0:T(8,128)S(1)}, u32[]{:S(2)}, u32[]{:S(2)}) collective-permute-start(f32[2,256,256]{2,1,0:T(8,128)S(1)} %get-tuple-element.6), channel_id=1, source_target_pairs={{0,16},{8,24},{16,0},{24,8},{1,17},{9,25},{17,1},{25,9},{2,18},{10... | collective-permute-start | bytes 1572872 | tf_op jit(solution)/shard_map/ppermute | solution.py:21
  50.7 10.5 %copy-start.1 = (f32[4096,256]{1,0:T(8,128)S(1)}, f32[4096,256]{1,0:T(8,128)}, u32[]{:S(2)}) copy-start(f32[4096,256]{1,0:T(8,128)} %all-gather.3.cloned.1.call-done) | copy-start | bytes 12582916
  69.3 2.7 %copy-start = (f32[4096,384]{0,1:T(8,128)}, f32[4096,384]{0,1:T(8,128)S(1)}, u32[]{:S(2)}) copy-start(f32[4096,384]{0,1:T(8,128)S(1)} %bitcast_subtract_fusion) | copy-start | bytes 18874372
  72.1 26.5 %collective-permute-start = (f32[256,384]{0,1:T(8,128)S(1)}, f32[256,384]{0,1:T(8,128)S(1)}, u32[]{:S(2)}, u32[]{:S(2)}) collective-permute-start(f32[256,384]{0,1:T(8,128)S(1)} %slice.8), channel_id=1, source_target_pairs={{0,8},{8,0},{16,24},{24,16},{1,9},{9,1},{17,25},{25,17},{2,10},{10... | collective-permute-start | bytes 1179656 | tf_op jit(solution)/shard_map/ppermute | solution.py:33
  102.6 20.3 %collective-permute-start.3 = (f32[256,384]{0,1:T(8,128)S(1)}, f32[256,384]{0,1:T(8,128)S(1)}, u32[]{:S(2)}, u32[]{:S(2)}) collective-permute-start(f32[256,384]{0,1:T(8,128)S(1)} %fusion.14), channel_id=1, source_target_pairs={{0,16},{8,24},{16,0},{24,8},{1,17},{9,25},{17,1},{25,9},{2,18},{10... | collective-permute-start | bytes 1179656 | tf_op jit(solution)/shard_map/ppermute | solution.py:33
  103.1 5.7 %copy-start.2 = (f32[1024,256]{1,0:T(8,128)S(1)}, f32[1024,256]{1,0:T(8,128)}, u32[]{:S(2)}) copy-start(f32[1024,256]{1,0:T(8,128)} %all-gather.5.cloned.1.call-done) | copy-start | bytes 3145732
Sparse Core Ops, SparseCore 0:
  9.2 41.4 all-gather.2
  52.2 40.9 all-gather.4
